TPU v7x, 32 devices: a whole 2x2x4 slice. The times are simulated.
32 devices in a mesh: dp: 4 (over y, x), expert: 8 (over z, core).
Axes of the slice: x: 2, y: 2, z: 4, core: 2. Of those that a mesh axis runs over, the one named last changes fastest.
Arguments:
- images: bfloat16 [32, 197, 768], P(('dp', 'expert')), may hold values from -6 to 6
- ln1_gain: bfloat16 [768], P(('dp', 'expert')), may hold values from 0.25 to 1.75
- ln1_bias: bfloat16 [768], P(('dp', 'expert')), may hold values from -3 to 3
- qkv_weight: bfloat16 [768, 2304], P(('dp', 'expert')), may hold values from -0.21875 to 0.21875
- q_bias: bfloat16 [768], P(('dp', 'expert')), may hold values from -3 to 3
- v_bias: bfloat16 [768], P(('dp', 'expert')), may hold values from -3 to 3
- out_weight: bfloat16 [768, 768], P(('dp', 'expert')), may hold values from -0.875 to 0.875
- out_bias: bfloat16 [768], P(('dp', 'expert')), may hold values from -3 to 3
- ln2_gain: bfloat16 [768], P(('dp', 'expert')), may hold values from 0.25 to 1.75
- ln2_bias: bfloat16 [768], P(('dp', 'expert')), may hold values from -3 to 3
- in_weight: bfloat16 [8, 768, 3072], P('expert'), may hold values from -0.21875 to 0.21875
- in_bias: bfloat16 [8, 3072], P('expert'), may hold values from -3 to 3
- down_weight: bfloat16 [8, 3072, 768], P('expert'), may hold values from -0.109375 to 0.109375
- down_bias: bfloat16 [8, 768], P('expert'), may hold values from -3 to 3
- routes: int32 [32, 197, 2], P(('dp', 'expert')), may hold values from 0 to 7, all different within a row; in each aligned block of 197 rows (0 to 196, 197 to 393, ..., all dimensions but the last counted through in order) at most 50 rows name the same one
- gate_weights: float32 [32, 197, 2], P(('dp', 'expert')), may hold values from 0.1 to 1
- grad_out: bfloat16 [32, 197, 768], P(('dp', 'expert')), may hold values from -6 to 6
Outputs:
- block_output: bfloat16 [32, 197, 768], P(('dp', 'expert'))
- image_grad: float32 [32, 197, 768], P(('dp', 'expert'))
- ln1_gain_grad: float32 [768], P(('dp', 'expert'))
- ln1_bias_grad: float32 [768], P(('dp', 'expert'))
- qkv_weight_grad: float32 [768, 2304], P(('dp', 'expert'))
- q_bias_grad: float32 [768], P(('dp', 'expert'))
- v_bias_grad: float32 [768], P(('dp', 'expert'))
- out_weight_grad: float32 [768, 768], P(('dp', 'expert'))
- out_bias_grad: float32 [768], P(('dp', 'expert'))
- ln2_gain_grad: float32 [768], P(('dp', 'expert'))
- ln2_bias_grad: float32 [768], P(('dp', 'expert'))
- in_weight_grad: float32 [8, 768, 3072], P('expert', None, 'dp')
- in_bias_grad: float32 [8, 3072], P('expert', 'dp')
- down_weight_grad: float32 [8, 3072, 768], P('expert', 'dp')
- down_bias_grad: float32 [8, 768], P('expert', 'dp')
Inputs may be any that keep to these rules, and one draw needn't show every extreme that they name: `routes`: in each aligned block of 197 rows (the tokens of one device) no expert is named more than 50 times, a bound that some block reaches; the two experts of a token differ.
All inputs are finite; a program needn't handle non-finite values.
Results may differ from a plain program's by a relative error of at most 0.012.
Values may be sent and summed in bfloat16 or wider, within the bound.
No kernel may reach another device: no remote copies, remote signals or barrier semaphores. Data moves between devices by JAX's collectives and lax.ppermute only.
A program may use at most 192 MiB of HBM per device.

v0:
```python
import jax
import jax.numpy as jnp
from jax import lax
from jax.sharding import PartitionSpec as P

D = 768
HEADS = 12
HEAD_DIM = 64
SEQ = 197
EPSILON = 1e-06


def to_half(values):
    return lax.optimization_barrier(values.astype(jnp.bfloat16))


def layer_norm(values, gain, shift):
    average = jnp.mean(values, axis=-1, keepdims=True)
    centred = values - average
    inverse = lax.rsqrt(jnp.mean(centred * centred, axis=-1, keepdims=True) + EPSILON)
    normal = centred * inverse
    return (normal * gain.astype(jnp.float32) + shift.astype(jnp.float32), normal, inverse)


def norm_back(upstream, normal, inverse, gain):
    weighted = upstream * gain.astype(jnp.float32)
    first_mean = jnp.mean(weighted, axis=-1, keepdims=True)
    second_mean = jnp.mean(weighted * normal, axis=-1, keepdims=True)
    return inverse * (weighted - first_mean - normal * second_mean)


def slot_positions(flat_routes, expert_count, capacity):
    onehot = (flat_routes[:, None] == jnp.arange(expert_count, dtype=jnp.int32)[None, :]).astype(
        jnp.int32
    )
    earlier = jnp.cumsum(onehot, axis=0) - onehot
    return flat_routes * capacity + jnp.sum(earlier * onehot, axis=1)


def split_heads(projected, image_count):
    parts = projected.reshape(image_count, SEQ, 3, HEADS, HEAD_DIM)
    return (parts[:, :, 0], parts[:, :, 1], parts[:, :, 2])


def head_scores(queries, key_heads):
    return jnp.einsum(
        "bqhd,bkhd->bhqk", queries, key_heads, preferred_element_type=jnp.float32
    ) * HEAD_DIM ** (-0.5)


def per_device(
    images,
    ln1_gain,
    ln1_bias,
    qkv_weight,
    q_bias,
    v_bias,
    out_weight,
    out_bias,
    ln2_gain,
    ln2_bias,
    in_weight,
    in_bias,
    down_weight,
    down_bias,
    routes,
    gate_weights,
    grad_out,
):
    gathered = (
        lax.all_gather(ln1_gain, ("dp", "expert"), axis=0, tiled=True),
        lax.all_gather(ln1_bias, ("dp", "expert"), axis=0, tiled=True),
        lax.all_gather(qkv_weight, ("dp", "expert"), axis=0, tiled=True),
        lax.all_gather(q_bias, ("dp", "expert"), axis=0, tiled=True),
        lax.all_gather(v_bias, ("dp", "expert"), axis=0, tiled=True),
        lax.all_gather(out_weight, ("dp", "expert"), axis=0, tiled=True),
        lax.all_gather(out_bias, ("dp", "expert"), axis=0, tiled=True),
        lax.all_gather(ln2_gain, ("dp", "expert"), axis=0, tiled=True),
        lax.all_gather(ln2_bias, ("dp", "expert"), axis=0, tiled=True),
    )
    (
        full_gain_one,
        full_bias_one,
        full_qkv,
        full_q_bias,
        full_v_bias,
        full_out,
        full_out_bias,
        full_gain_two,
        full_bias_two,
    ) = gathered
    image_count = images.shape[0]
    token_count = image_count * SEQ
    inputs = images.reshape(token_count, D).astype(jnp.float32)
    normed_one, normal_one, inverse_one = layer_norm(inputs, full_gain_one, full_bias_one)
    normed_one = to_half(normed_one)
    bias_row = jnp.concatenate(
        [
            full_q_bias.astype(jnp.float32),
            jnp.zeros((D,), jnp.float32),
            full_v_bias.astype(jnp.float32),
        ]
    )
    projected = to_half(
        jnp.dot(normed_one, full_qkv, preferred_element_type=jnp.float32) + bias_row
    )
    queries, key_heads, value_heads = split_heads(projected, image_count)
    scores = head_scores(queries, key_heads)
    log_total = jnp.log(jnp.sum(jnp.exp(scores), axis=-1, keepdims=True))
    attention = to_half(jnp.exp(scores - log_total))
    context = jnp.einsum(
        "bhqk,bkhd->bqhd", attention, value_heads, preferred_element_type=jnp.float32
    )
    context = context.astype(jnp.bfloat16).reshape(token_count, D)
    residual = (
        inputs
        + jnp.dot(context, full_out, preferred_element_type=jnp.float32)
        + full_out_bias.astype(jnp.float32)
    )
    normed_two, normal_two, inverse_two = layer_norm(residual, full_gain_two, full_bias_two)
    normed_two = to_half(normed_two)
    expert_count = lax.axis_size("expert")
    capacity = max(2, (2 * token_count + expert_count - 1) // expert_count)
    slot_total = expert_count * capacity
    positions = slot_positions(routes.reshape(2 * token_count), expert_count, capacity)
    mixing = gate_weights.reshape(2 * token_count, 1)
    outgoing = (
        jnp.zeros((slot_total, D), jnp.bfloat16)
        .at[positions]
        .set(jnp.repeat(normed_two, 2, axis=0))
    )
    received = lax.all_to_all(
        outgoing.reshape(expert_count, capacity, D),
        "expert",
        split_axis=0,
        concat_axis=0,
        tiled=True,
    ).reshape(slot_total, D)
    weight_in = in_weight[0]
    weight_down = down_weight[0]
    hidden_pre = jnp.dot(received, weight_in, preferred_element_type=jnp.float32) + in_bias[
        0
    ].astype(jnp.float32)
    activated = to_half(jax.nn.gelu(hidden_pre))
    expert_result = to_half(
        jnp.dot(activated, weight_down, preferred_element_type=jnp.float32)
        + down_bias[0].astype(jnp.float32)
    )
    returned = lax.all_to_all(
        expert_result.reshape(expert_count, capacity, D),
        "expert",
        split_axis=0,
        concat_axis=0,
        tiled=True,
    ).reshape(slot_total, D)
    picked = returned[positions].astype(jnp.float32)
    mixture = jnp.sum((picked * mixing).reshape(token_count, 2, D), axis=1)
    block_output = (residual + mixture).astype(jnp.bfloat16).reshape(images.shape)
    upstream = grad_out.reshape(token_count, D).astype(jnp.float32)
    routed_grads = to_half(jnp.repeat(upstream, 2, axis=0) * mixing)
    grad_buffer = jnp.zeros((slot_total, D), jnp.bfloat16).at[positions].set(routed_grads)
    routed_in = lax.all_to_all(
        grad_buffer.reshape(expert_count, capacity, D),
        "expert",
        split_axis=0,
        concat_axis=0,
        tiled=True,
    ).reshape(slot_total, D)
    grad_hidden = jnp.dot(routed_in, weight_down.T, preferred_element_type=jnp.float32)
    grad_pre = to_half(jax.vjp(jax.nn.gelu, hidden_pre)[1](grad_hidden)[0])
    grad_rows = to_half(jnp.dot(grad_pre, weight_in.T, preferred_element_type=jnp.float32))
    grad_returned = lax.all_to_all(
        grad_rows.reshape(expert_count, capacity, D),
        "expert",
        split_axis=0,
        concat_axis=0,
        tiled=True,
    ).reshape(slot_total, D)
    local_in = jnp.dot(received.T, grad_pre, preferred_element_type=jnp.float32)
    local_down = jnp.dot(activated.T, routed_in, preferred_element_type=jnp.float32)
    local_bias_in = jnp.sum(grad_pre.astype(jnp.float32), axis=0)
    local_bias_down = jnp.sum(routed_in.astype(jnp.float32), axis=0)
    grad_weight_in, grad_weight_down, grad_bias_in, grad_bias_down = (
        lax.psum_scatter(
            local_in.astype(jnp.bfloat16), "dp", scatter_dimension=1, tiled=True
        ).astype(jnp.float32),
        lax.psum_scatter(
            local_down.astype(jnp.bfloat16), "dp", scatter_dimension=0, tiled=True
        ).astype(jnp.float32),
        lax.psum_scatter(
            local_bias_in.astype(jnp.bfloat16), "dp", scatter_dimension=0, tiled=True
        ).astype(jnp.float32),
        lax.psum_scatter(
            local_bias_down.astype(jnp.bfloat16), "dp", scatter_dimension=0, tiled=True
        ).astype(jnp.float32),
    )
    grad_normed_two = jnp.sum(
        grad_returned[positions].astype(jnp.float32).reshape(token_count, 2, D), axis=1
    )
    ln2_gain_grad = jnp.sum(grad_normed_two * normal_two, axis=0)
    ln2_bias_grad = jnp.sum(grad_normed_two, axis=0)
    grad_residual = upstream + norm_back(grad_normed_two, normal_two, inverse_two, full_gain_two)
    out_bias_grad = jnp.sum(grad_residual, axis=0)
    branch_grad = to_half(grad_residual)
    out_weight_grad = jnp.dot(context.T, branch_grad, preferred_element_type=jnp.float32)
    grad_context = to_half(jnp.dot(branch_grad, full_out.T, preferred_element_type=jnp.float32))
    probable = jnp.exp(head_scores(queries, key_heads) - log_total)
    incoming = grad_context.reshape(image_count, SEQ, HEADS, HEAD_DIM)
    grad_values = jnp.einsum(
        "bhqk,bqhd->bkhd", attention, incoming, preferred_element_type=jnp.float32
    )
    grad_probs = jnp.einsum(
        "bqhd,bkhd->bhqk", incoming, value_heads, preferred_element_type=jnp.float32
    )
    centre = jnp.sum(probable * grad_probs, axis=-1, keepdims=True)
    grad_scores = to_half(probable * (grad_probs - centre) * HEAD_DIM ** (-0.5))
    grad_queries = jnp.einsum(
        "bhqk,bkhd->bqhd", grad_scores, key_heads, preferred_element_type=jnp.float32
    )
    grad_keys = jnp.einsum(
        "bhqk,bqhd->bkhd", grad_scores, queries, preferred_element_type=jnp.float32
    )
    grad_projected = jnp.stack([grad_queries, grad_keys, grad_values], axis=2).reshape(
        token_count, 3 * D
    )
    q_bias_grad = jnp.sum(grad_projected[:, :D], axis=0)
    v_bias_grad = jnp.sum(grad_projected[:, 2 * D :], axis=0)
    projected_grad = to_half(grad_projected)
    qkv_weight_grad = jnp.dot(normed_one.T, projected_grad, preferred_element_type=jnp.float32)
    grad_normed_one = jnp.dot(projected_grad, full_qkv.T, preferred_element_type=jnp.float32)
    ln1_gain_grad = jnp.sum(grad_normed_one * normal_one, axis=0)
    ln1_bias_grad = jnp.sum(grad_normed_one, axis=0)
    image_grad = (
        grad_residual + norm_back(grad_normed_one, normal_one, inverse_one, full_gain_one)
    ).reshape(images.shape)
    summed = (
        lax.psum_scatter(ln1_gain_grad, ("dp", "expert"), scatter_dimension=0, tiled=True),
        lax.psum_scatter(ln1_bias_grad, ("dp", "expert"), scatter_dimension=0, tiled=True),
        lax.psum_scatter(qkv_weight_grad, ("dp", "expert"), scatter_dimension=0, tiled=True),
        lax.psum_scatter(q_bias_grad, ("dp", "expert"), scatter_dimension=0, tiled=True),
        lax.psum_scatter(v_bias_grad, ("dp", "expert"), scatter_dimension=0, tiled=True),
        lax.psum_scatter(out_weight_grad, ("dp", "expert"), scatter_dimension=0, tiled=True),
        lax.psum_scatter(out_bias_grad, ("dp", "expert"), scatter_dimension=0, tiled=True),
        lax.psum_scatter(ln2_gain_grad, ("dp", "expert"), scatter_dimension=0, tiled=True),
        lax.psum_scatter(ln2_bias_grad, ("dp", "expert"), scatter_dimension=0, tiled=True),
    )
    (
        gain_one_share,
        bias_one_share,
        qkv_share,
        q_bias_share,
        v_bias_share,
        out_share,
        out_bias_share,
        gain_two_share,
        bias_two_share,
    ) = summed
    return (
        block_output,
        image_grad,
        gain_one_share,
        bias_one_share,
        qkv_share,
        q_bias_share,
        v_bias_share,
        out_share,
        out_bias_share,
        gain_two_share,
        bias_two_share,
        grad_weight_in[None],
        grad_bias_in[None],
        grad_weight_down[None],
        grad_bias_down[None],
    )


def solution(mesh):
    in_specs = (
        P(("dp", "expert"), None, None),
        P(("dp", "expert")),
        P(("dp", "expert")),
        P(("dp", "expert"), None),
        P(("dp", "expert")),
        P(("dp", "expert")),
        P(("dp", "expert"), None),
        P(("dp", "expert")),
        P(("dp", "expert")),
        P(("dp", "expert")),
        P("expert", None, None),
        P("expert", None),
        P("expert", None, None),
        P("expert", None),
        P(("dp", "expert"), None, None),
        P(("dp", "expert"), None, None),
        P(("dp", "expert"), None, None),
    )
    out_specs = (
        P(("dp", "expert"), None, None),
        P(("dp", "expert"), None, None),
        P(("dp", "expert")),
        P(("dp", "expert")),
        P(("dp", "expert"), None),
        P(("dp", "expert")),
        P(("dp", "expert")),
        P(("dp", "expert"), None),
        P(("dp", "expert")),
        P(("dp", "expert")),
        P(("dp", "expert")),
        P("expert", None, "dp"),
        P("expert", "dp"),
        P("expert", "dp", None),
        P("expert", "dp"),
    )
    return jax.shard_map(
        per_device, mesh=mesh, in_specs=in_specs, out_specs=out_specs, check_vma=False
    )
```

profile of v0, /device:TPU:0, one launch (start us, length us, event | category | flops | bytes accessed | tf_op | source)
XLA Modules:
  0.0 538.8 jit_solution(14895257947561775607)
XLA Ops:
  14.2 2.3 scatter_custom_fusion.1
  17.6 6.4 %all-to-all-start.2 = ((bf16[8,50,768]{2,1,0:T(8,128)(2,1)}), bf16[8,50,768]{2,1,0:T(8,128)(2,1)}, u32[]{:S(2)}, u32[]{:S(2)}) async-start(bf16[8,50,768]{2,1,0:T(8,128)(2,1)} %reshape.261), calls=%async_computation.2 | async-start | bytes 1376256 | tf_op jit(solution)/shard_map/all_to_all | solution.py:162
  26.3 42.0 %all-reduce.18 = (bf16[768]{0:T(1024)(128)(2,1)S(1)}, bf16[768]{0:T(1024)(128)(2,1)S(1)}, bf16[768]{0:T(1024)(128)(2,1)S(1)}, bf16[768]{0:T(1024)(128)(2,1)S(1)}...) all-reduce(bf16[768]{0:T(1024)(128)(2,1)S(1)} %dynamic-update-slice, ...), channel_id=1, replica_groups=mesh['dp'=4,'expert'=8] {'dp','expert'}, use_global_device_ids=true, to_apply=%add.2 | all-reduce | flops 5376 | bytes 21504
  69.1 6.3 %all-gather.3.cloned.1.call-done = bf16[768,2304]{1,0:T(8,128)(2,1)} async-done(((bf16[24,2304]{1,0:T(8,128)(2,1)}), bf16[768,2304]{1,0:T(8,128)(2,1)}) %all-gather.3.cloned.1.call-update) | async-done | bytes 3538960 | tf_op jit(solution)/shard_map/all_gather | solution.py:73
  75.4 2.9 fusion.17
  80.5 2.1 fusion.20
  83.7 1.3 convolution_convert_fusion.2
  85.1 46.3 %all-gather.5.cloned.1.call-done = bf16[768,768]{1,0:T(8,128)(2,1)} async-done(((bf16[24,768]{1,0:T(8,128)(2,1)}), bf16[768,768]{1,0:T(8,128)(2,1)}) %all-gather.5.cloned.1.call-update) | async-done | bytes 1179664 | tf_op jit(solution)/shard_map/all_gather | solution.py:76
  131.4 1.8 fusion.75
  136.0 2.7 reshape.299
  138.6 2.9 scatter_custom_fusion
  142.5 3.5 all-to-all-start
  146.7 2.1 reshape.262
  148.8 16.1 %all-to-all-done = bf16[8,50,768]{2,1,0:T(8,128)(2,1)S(1)} async-done(((bf16[8,50,768]{2,1,0:T(8,128)(2,1)}), bf16[8,50,768]{2,1,0:T(8,128)(2,1)S(1)}, u32[]{:S(2)}, u32[]{:S(2)}) %all-to-all-start) | async-done | bytes 614432 | tf_op jit(solution)/shard_map/all_to_all | solution.py:132
  165.8 7.2 %multiply_convert_fusion = (bf16[400,3072]{1,0:T(8,128)(2,1)}, f32[400,3072]{1,0:T(8,128)S(1)}) fusion(f32[3072]{0:T(1024)S(1)} %bitcast.175, bf16[400,768]{1,0:T(8,128)(2,1)} %reshape.256, bf16[1,768,3072]{2,1,0:T(8,128)(2,1)} %param.27), kind=kOutput, calls=%fused_computation.17 | convolution fusion | flops 1899724800 | bytes 12718080 | tf_op jit(solution)/shard_map/dot_general | solution.py:141
  173.1 7.5 %fusion.8 = bf16[400,3072]{1,0:T(8,128)(2,1)S(1)} fusion(f32[400,3072]{1,0:T(8,128)S(1)} %get-tuple-element.91, bf16[400,768]{1,0:T(8,128)(2,1)S(1)} %copy-done.19, bf16[1,3072,768]{2,1,0:T(8,128)(2,1)} %param.29, f32[3072]{0:T(1024)S(1)} %bitcast.176), kind=kOutput, calls=%fused_computation.16 | convolution fusion | flops 1913241600 | bytes 12718080 | tf_op jit(solution)/shard_map/dot_general | solution.py:169
  180.6 1.5 copy-done.15
  182.1 4.3 convolution_convert_fusion.1
  186.5 6.5 %convolution_convert_fusion = bf16[3072,768]{1,0:T(8,128)(2,1)} fusion(bf16[400,3072]{1,0:T(8,128)(2,1)} %get-tuple-element.90, bf16[400,768]{1,0:T(8,128)(2,1)S(1)} %copy-done.19), kind=kOutput, calls=%fused_computation.8 | convolution fusion | flops 1889796096 | bytes 7790592 | tf_op jit(solution)/shard_map/dot_general | solution.py:180
  193.0 5.2 fusion.37
  199.2 3.7 all-to-all-start.3
  203.0 6.3 %fusion.34 = bf16[400,768]{1,0:T(8,128)(2,1)} fusion(bf16[400,3072]{1,0:T(8,128)(2,1)} %get-tuple-element.90, bf16[1,3072,768]{2,1,0:T(8,128)(2,1)} %param.29, f32[768]{0:T(1024)S(1)} %convert_reduce_fusion.2), kind=kOutput, calls=%fused_computation.39 | convolution fusion | flops 1888051200 | bytes 7793664 | tf_op jit(solution)/shard_map/dot_general | solution.py:146
  209.3 2.1 reshape.257
  211.4 10.3 %all-to-all-done.3 = bf16[8,50,768]{2,1,0:T(8,128)(2,1)S(1)} async-done(((bf16[8,50,768]{2,1,0:T(8,128)(2,1)}), bf16[8,50,768]{2,1,0:T(8,128)(2,1)S(1)}, u32[]{:S(2)}, u32[]{:S(2)}) %all-to-all-start.3) | async-done | bytes 614432 | tf_op jit(solution)/shard_map/all_to_all | solution.py:172
  221.7 4.2 all-to-all-start.1
  226.8 1.3 pad_clamp_fusion
  229.3 2.8 gather_fusion.1
  232.1 2.8 reshape.274
  234.9 3.6 reduce_sum.214
  238.5 6.3 %all-to-all-done.1 = bf16[8,50,768]{2,1,0:T(8,128)(2,1)} async-done(((bf16[8,50,768]{2,1,0:T(8,128)(2,1)}), bf16[8,50,768]{2,1,0:T(8,128)(2,1)}, u32[]{:S(2)}, u32[]{:S(2)}) %all-to-all-start.1) | async-done | bytes 614432 | tf_op jit(solution)/shard_map/all_to_all | solution.py:149
  246.1 2.7 gather_fusion
  248.7 2.8 reshape.272
  251.6 2.3 multiply_reduce_fusion.2
  253.9 2.8 multiply_reduce_fusion.1
  258.6 1.9 fusion.77
  260.8 1.9 convolution_convert_fusion.3
  262.9 3.1 fusion.28
  266.0 2.0 convolution_bitcast_fusion
  270.4 4.1 fusion.76
  278.3 2.1 reduce_sum.227
  280.4 10.0 %all-reduce.19 = (bf16[3072]{0:T(1024)(128)(2,1)S(1)}, bf16[768]{0:T(1024)(128)(2,1)S(1)}) all-reduce(bf16[3072]{0:T(1024)(128)(2,1)S(1)} %reduce_sum.227, bf16[768]{0:T(1024)(128)(2,1)S(1)} %reduce_sum.228), channel_id=12, replica_groups=mesh['dp'=4,'expert'=8] {'dp'}, use_global_device_ids=true, to_apply=%region_35.36.clone | all-reduce | flops 3840 | bytes 15360
  291.7 4.0 fusion.60
  296.0 1.4 copy.64
  297.9 37.3 %all-reduce.17 = (f32[768]{0:T(1024)S(1)}, f32[768]{0:T(1024)S(1)}, f32[768]{0:T(1024)S(1)}, f32[768]{0:T(1024)S(1)}, f32[768]{0:T(1024)S(1)}, /*index=5*/f32[768]{0:T(1024)S(1)}, f32[768]{0:T(1024)S(1)}) all-reduce(f32[768]{0:T(1024)S(1)} %get-tuple-element.64, ...), channel_id=2, replica_groups=mesh['dp'=4,'expert'=8] {'dp','expert'}, use_global_device_ids=true, to_apply=%region_18.19.clone | all-reduce | flops 5376 | bytes 43008
  339.3 2.9 bitcast_convert_fusion.1
  342.2 2.9 bitcast_convert_fusion
  345.0 61.9 %reduce-scatter.7.cloned.1.call-done = f32[24,768]{1,0:T(8,128)} async-done(((f32[768,768]{1,0:T(8,128)}), f32[24,768]{1,0:T(8,128)}) %reduce-scatter.7.cloned.1.call-update) | async-done | bytes 73744 | tf_op jit(solution)/shard_map/reduce_scatter | solution.py:242
  406.9 124.8 %reduce-scatter.5.cloned.1.call-done = f32[24,2304]{1,0:T(8,128)} async-done(((f32[768,2304]{1,0:T(8,128)}), f32[24,2304]{1,0:T(8,128)}) %reduce-scatter.5.cloned.1.call-update) | async-done | bytes 221200 | tf_op jit(solution)/shard_map/reduce_scatter | solution.py:239
  (198 shorter events, 37.2 us)
Async XLA Ops:
  7.2 68.2 %all-gather.3.cloned.1.call-start = ((), (), s32[]{:S(2)}) async-start(), calls=%async_computation.8 | async-start | bytes 3649536 | tf_op jit(solution)/shard_map/all_gather | solution.py:73
  11.3 2.3 copy-start.36
  13.8 10.9 %copy-start.39 = (bf16[24]{0:T(256)(128)(2,1)S(1)}, bf16[24]{0:T(256)(128)(2,1)}, u32[]{:S(2)}) copy-start(bf16[24]{0:T(256)(128)(2,1)} %param.19) | copy-start | bytes 148
  13.8 11.1 %copy-start.40 = (bf16[24]{0:T(256)(128)(2,1)S(1)}, bf16[24]{0:T(256)(128)(2,1)}, u32[]{:S(2)}) copy-start(bf16[24]{0:T(256)(128)(2,1)} %param.18) | copy-start | bytes 148
  13.9 11.3 %copy-start.41 = (bf16[24]{0:T(256)(128)(2,1)S(1)}, bf16[24]{0:T(256)(128)(2,1)}, u32[]{:S(2)}) copy-start(bf16[24]{0:T(256)(128)(2,1)} %param.22) | copy-start | bytes 148
  13.9 11.5 %copy-start.42 = (bf16[24]{0:T(256)(128)(2,1)S(1)}, bf16[24]{0:T(256)(128)(2,1)}, u32[]{:S(2)}) copy-start(bf16[24]{0:T(256)(128)(2,1)} %param.21) | copy-start | bytes 148
  13.9 11.8 %copy-start.43 = (bf16[24]{0:T(256)(128)(2,1)S(1)}, bf16[24]{0:T(256)(128)(2,1)}, u32[]{:S(2)}) copy-start(bf16[24]{0:T(256)(128)(2,1)} %param.24) | copy-start | bytes 148
  13.9 12.0 %copy-start.44 = (bf16[24]{0:T(256)(128)(2,1)S(1)}, bf16[24]{0:T(256)(128)(2,1)}, u32[]{:S(2)}) copy-start(bf16[24]{0:T(256)(128)(2,1)} %param.26) | copy-start | bytes 148
  13.9 12.2 %copy-start.45 = (bf16[24]{0:T(256)(128)(2,1)S(1)}, bf16[24]{0:T(256)(128)(2,1)}, u32[]{:S(2)}) copy-start(bf16[24]{0:T(256)(128)(2,1)} %param.25) | copy-start | bytes 148
  13.9 54.4 %copy-start.6 = (bf16[1,197,768]{2,1,0:T(8,128)(2,1)S(1)}, bf16[1,197,768]{2,1,0:T(8,128)(2,1)}, u32[]{:S(2)}) copy-start(bf16[1,197,768]{2,1,0:T(8,128)(2,1)} %param.17) | copy-start | bytes 907780
  14.2 124.4 %copy-start.37 = (s32[394,1]{0,1:T(1,128)}, s32[394,1]{0,1:T(1,128)S(1)}, u32[]{:S(2)}) copy-start(s32[394,1]{0,1:T(1,128)S(1)} %compare_select_fusion) | copy-start | bytes 4732
  17.6 124.9 %all-to-all-start.2 = ((bf16[8,50,768]{2,1,0:T(8,128)(2,1)}), bf16[8,50,768]{2,1,0:T(8,128)(2,1)}, u32[]{:S(2)}, u32[]{:S(2)}) async-start(bf16[8,50,768]{2,1,0:T(8,128)(2,1)} %reshape.261), calls=%async_computation.2 | async-start | bytes 1376256 | tf_op jit(solution)/shard_map/all_to_all | solution.py:162
  23.9 107.5 %all-gather.5.cloned.1.call-start = ((), (), s32[]{:S(2)}) async-start(), calls=%async_computation.9 | async-start | bytes 1216512 | tf_op jit(solution)/shard_map/all_gather | solution.py:76
  68.8 6.6 %copy-start.34 = (f32[197]{0:T(256)}, f32[197]{0:T(256)S(1)}, u32[]{:S(2)}) copy-start(f32[197]{0:T(256)S(1)} %add_rsqrt_fusion.1) | copy-start | bytes 2368
  69.0 6.4 %copy-start.16 = (bf16[197,768]{1,0:T(8,128)(2,1)}, bf16[197,768]{1,0:T(8,128)(2,1)S(1)}, u32[]{:S(2)}) copy-start(bf16[197,768]{1,0:T(8,128)(2,1)S(1)} %fusion.54) | copy-start | bytes 907780
  69.1 64.4 %copy-start.21 = (f32[768]{0:T(1024)}, f32[768]{0:T(1024)S(1)}, u32[]{:S(2)}) copy-start(f32[768]{0:T(1024)S(1)} %convert_element_type.146) | copy-start | bytes 9220
  82.7 1.0 copy-start.5
  85.1 50.9 %copy-start.12 = (bf16[12,64,197]{2,1,0:T(8,128)(2,1)}, bf16[12,64,197]{2,1,0:T(8,128)(2,1)S(1)}, u32[]{:S(2)}) copy-start(bf16[12,64,197]{2,1,0:T(8,128)(2,1)S(1)} %convolution_convert_fusion.2) | copy-start | bytes 907780
  136.0 10.7 %copy-start.33 = (bf16[1,3072]{1,0:T(2,128)(2,1)S(1)}, bf16[1,3072]{1,0:T(2,128)(2,1)}, u32[]{:S(2)}) copy-start(bf16[1,3072]{1,0:T(2,128)(2,1)} %param.28) | copy-start | bytes 18436
  142.5 22.3 %all-to-all-start = ((bf16[8,50,768]{2,1,0:T(8,128)(2,1)}), bf16[8,50,768]{2,1,0:T(8,128)(2,1)S(1)}, u32[]{:S(2)}, u32[]{:S(2)}) async-start(bf16[8,50,768]{2,1,0:T(8,128)(2,1)} %reshape.255), calls=%async_computation | async-start | bytes 1376256 | tf_op jit(solution)/shard_map/all_to_all | solution.py:132
  146.1 193.2 %reduce-scatter.9.cloned.1.call-start = ((), (), s32[]{:S(2)}) async-start(), calls=%async_computation.12 | async-start | bytes 5898240 | tf_op jit(solution)/shard_map/reduce_scatter | solution.py:184
  165.8 7.2 %copy-start.19 = (bf16[400,768]{1,0:T(8,128)(2,1)S(1)}, bf16[400,768]{1,0:T(8,128)(2,1)}, u32[]{:S(2)}) copy-start(bf16[400,768]{1,0:T(8,128)(2,1)} %reshape.262) | copy-start | bytes 1843204
  173.1 9.0 %copy-start.20 = (bf16[400,768]{1,0:T(8,128)(2,1)S(1)}, bf16[400,768]{1,0:T(8,128)(2,1)}, u32[]{:S(2)}) copy-start(bf16[400,768]{1,0:T(8,128)(2,1)} %reshape.256) | copy-start | bytes 1843204
  180.6 1.5 copy-start.15
  186.4 155.7 %reduce-scatter.11.cloned.1.call-start = ((), (), s32[]{:S(2)}) async-start(), calls=%async_computation.13 | async-start | bytes 5898240 | tf_op jit(solution)/shard_map/reduce_scatter | solution.py:187
  198.2 4.8 copy-start.38
  199.2 22.5 %all-to-all-start.3 = ((bf16[8,50,768]{2,1,0:T(8,128)(2,1)}), bf16[8,50,768]{2,1,0:T(8,128)(2,1)S(1)}, u32[]{:S(2)}, u32[]{:S(2)}) async-start(bf16[8,50,768]{2,1,0:T(8,128)(2,1)} %reshape.263), calls=%async_computation.3 | async-start | bytes 1376256 | tf_op jit(solution)/shard_map/all_to_all | solution.py:172
  221.7 5.1 copy-start.14
  221.7 23.1 %all-to-all-start.1 = ((bf16[8,50,768]{2,1,0:T(8,128)(2,1)}), bf16[8,50,768]{2,1,0:T(8,128)(2,1)}, u32[]{:S(2)}, u32[]{:S(2)}) async-start(bf16[8,50,768]{2,1,0:T(8,128)(2,1)} %reshape.257), calls=%async_computation.1 | async-start | bytes 1376256 | tf_op jit(solution)/shard_map/all_to_all | solution.py:149
  225.9 181.0 %reduce-scatter.7.cloned.1.call-start = ((), (), s32[]{:S(2)}) async-start(), calls=%async_computation.11 | async-start | bytes 2433024 | tf_op jit(solution)/shard_map/reduce_scatter | solution.py:242
  232.1 13.9 %copy-start.27 = (s32[1024]{0:T(1024)S(1)}, s32[1024]{0:T(1024)}, u32[]{:S(2)}) copy-start(s32[1024]{0:T(1024)} %pad_clamp_fusion) | copy-start | bytes 12292
  246.0 5.5 %copy-start.22 = (f32[768]{0:T(1024)S(1)}, f32[768]{0:T(1024)}, u32[]{:S(2)}) copy-start(f32[768]{0:T(1024)} %copy-done.21) | copy-start | bytes 9220
  246.1 5.5 %copy-start.26 = (f32[197]{0:T(256)S(1)}, f32[197]{0:T(256)}, u32[]{:S(2)}) copy-start(f32[197]{0:T(256)} %copy-done.25) | copy-start | bytes 2368
  246.1 5.5 %copy-start.31 = (f32[197]{0:T(256)S(1)}, f32[197]{0:T(256)}, u32[]{:S(2)}) copy-start(f32[197]{0:T(256)} %copy-done.30) | copy-start | bytes 2368
  248.7 8.0 %copy-start.1 = (f32[197,768]{1,0:T(8,128)S(1)}, f32[197,768]{1,0:T(8,128)}, u32[]{:S(2)}) copy-start(f32[197,768]{1,0:T(8,128)} %copy-done) | copy-start | bytes 1815556
  251.6 5.1 copy-start.7
  251.6 5.1 copy-start.18
  256.7 1.9 copy-start.13
  260.5 271.2 %reduce-scatter.5.cloned.1.call-start = ((), (), s32[]{:S(2)}) async-start(), calls=%async_computation.10 | async-start | bytes 7299072 | tf_op jit(solution)/shard_map/reduce_scatter | solution.py:239
  265.9 2.0 copy-start.3
  266.0 2.2 copy-start.4
  269.2 1.2 copy-start.17
  274.5 17.2 %copy-start.24 = (f32[768]{0:T(1024)S(1)}, f32[768]{0:T(1024)}, u32[]{:S(2)}) copy-start(f32[768]{0:T(1024)} %copy-done.23) | copy-start | bytes 9220
  274.5 17.2 %copy-start.29 = (f32[197]{0:T(256)S(1)}, f32[197]{0:T(256)}, u32[]{:S(2)}) copy-start(f32[197]{0:T(256)} %copy-done.28) | copy-start | bytes 2368
  274.5 17.2 %copy-start.35 = (f32[197]{0:T(256)S(1)}, f32[197]{0:T(256)}, u32[]{:S(2)}) copy-start(f32[197]{0:T(256)} %copy-done.34) | copy-start | bytes 2368
  291.7 4.0 copy-start.10
  295.7 1.8 copy-start.8
  295.8 2.1 copy-start.32
  (9 other events, 7.0 us)
Sparse Core Ops, SparseCore 0:
  11.0 64.3 all-gather.2
  78.4 52.9 all-gather.4
  186.6 54.9 reduce-scatter.8
  244.4 57.1 reduce-scatter.10
  307.3 99.6 reduce-scatter.6
  413.1 118.6 reduce-scatter.4
where the time goes:
time: 545 us; the launch traced here: 539 us
  waiting for transfers between devices  273 us (50%)
  blocking collectives  89.3 us (16%)
  matrix products  61.4 us (11%)
  local copies, waits for them, and re-layouts  51.2 us (9%)
  other arithmetic  28.2 us (5%)
  starting transfers between devices  18.8 us (3%)
  between operations  16.5 us (3%)
    reduce_scatter x1, waiting for transfers between devices, per_device(): lax.psum_scatter(qkv_weight_grad, ('dp', 'expert'), scatter_dimension=0,...  125 us
    unnamed x3, blocking collectives  89.3 us
    reduce_scatter x1, waiting for transfers between devices, per_device(): lax.psum_scatter(out_weight_grad, ('dp', 'expert'), scatter_dimension=0,...  61.9 us
    all_gather x1, waiting for transfers between devices, per_device(): lax.all_gather(out_weight, ('dp', 'expert'), axis=0, tiled=True)  46.3 us
    unnamed x119, local copies, waits for them, and re-layouts  16.2 us
    all_to_all x1, waiting for transfers between devices, per_device(): lax.all_to_all(outgoing.reshape(expert_count, capacity, D), 'expert', spl...  16.1 us
  transfers between devices with their start and end apart: 10, of which 7 were waited for; matrix products, arithmetic and copies ran while one was open for 21% of the time, Pallas kernels for 0%

commit v1 on v0

--- a/solution.py
+++ b/solution.py
@@ -8,6 +8,28 @@
 HEAD_DIM = 64
 SEQ = 197
 EPSILON = 1e-06
+
+
+def laid_out(blocks, dim):
+    dims = list(blocks.shape[1:])
+    dims[dim] *= blocks.shape[0]
+    return jnp.moveaxis(blocks, 0, dim).reshape(dims)
+
+
+def collected_by_bits(x, axis):
+    size = lax.axis_size(axis)
+    blocks = x[None]
+    for level in range(size.bit_length() - 1):
+        apart = 1 << level
+        other = lax.ppermute(blocks, axis, [(i, i ^ apart) for i in range(size)])
+        both = jnp.stack([blocks, other])
+        upper = lax.axis_index(axis) >> level & 1
+        blocks = jnp.where(upper == 0, both, both[::-1]).reshape(-1, *x.shape)
+    return blocks
+
+
+def gather_by_bits(array, axis, dim):
+    return laid_out(collected_by_bits(array, axis), dim)
 
 
 def to_half(values):
@@ -73,7 +95,7 @@
         lax.all_gather(qkv_weight, ("dp", "expert"), axis=0, tiled=True),
         lax.all_gather(q_bias, ("dp", "expert"), axis=0, tiled=True),
         lax.all_gather(v_bias, ("dp", "expert"), axis=0, tiled=True),
-        lax.all_gather(out_weight, ("dp", "expert"), axis=0, tiled=True),
+        gather_by_bits(out_weight, ("dp", "expert"), 0),
         lax.all_gather(out_bias, ("dp", "expert"), axis=0, tiled=True),
         lax.all_gather(ln2_gain, ("dp", "expert"), axis=0, tiled=True),
         lax.all_gather(ln2_bias, ("dp", "expert"), axis=0, tiled=True),

time: 545 us -> 518 us (0.950)
  waiting for transfers between devices: 273 us -> 235 us
  starting transfers between devices: 18.8 us -> 26.8 us
  blocking collectives: 89.3 us -> 95.7 us
    all_gather x1 -> x0, waiting for transfers between devices: 46.3 us -> none  [per_device(): lax.all_gather(out_weight, ('dp', 'expert'), axis=0, tiled=True)]
    ppermute x0 -> x5, waiting for transfers between devices: none -> 10.7 us  [collected_by_bits(): other = lax.ppermute(blocks, axis, [(i, i ^ apart) for i in range(size)])]
    ppermute x0 -> x5, starting transfers between devices: none -> 9.03 us  [collected_by_bits(): other = lax.ppermute(blocks, axis, [(i, i ^ apart) for i in range(size)])]
    unnamed x3, blocking collectives: 89.3 us -> 95.7 us
    all_gather x1, waiting for transfers between devices: 6.28 us -> 0.01 us  [per_device(): lax.all_gather(qkv_weight, ('dp', 'expert'), axis=0, tiled=True)]
    unnamed x119 -> x91, local copies, waits for them, and re-layouts: 16.2 us -> 14.5 us
  transfers between devices with their start and end apart: 10 -> 14, of which waited for: 7 -> 8; matrix products, arithmetic and copies ran while one was open for 21% -> 22% of each run, Pallas kernels for 0% -> 0%
where the time goes in v1:
time: 518 us; the launch traced here: 510 us
  waiting for transfers between devices  235 us (45%)
  blocking collectives  95.7 us (18%)
  matrix products  60.7 us (12%)
  local copies, waits for them, and re-layouts  48.8 us (9%)
  other arithmetic  27.4 us (5%)
  starting transfers between devices  26.8 us (5%)
  between operations  16.4 us (3%)
    reduce_scatter x1, waiting for transfers between devices, per_device(): lax.psum_scatter(qkv_weight_grad, ('dp', 'expert'), scatter_dimension=0,...  125 us
    unnamed x3, blocking collectives  95.7 us
    reduce_scatter x1, waiting for transfers between devices, per_device(): lax.psum_scatter(out_weight_grad, ('dp', 'expert'), scatter_dimension=0,...  60.6 us
    all_to_all x1, waiting for transfers between devices, per_device(): lax.all_to_all(outgoing.reshape(expert_count, capacity, D), 'expert', spl...  17.3 us
    unnamed x91, local copies, waits for them, and re-layouts  14.5 us
    all_to_all x1, waiting for transfers between devices, per_device(): lax.all_to_all(grad_rows.reshape(expert_count, capacity, D), 'expert', sp...  12.3 us
    ppermute x5, waiting for transfers between devices, collected_by_bits(): other = lax.ppermute(blocks, axis, [(i, i ^ apart) for i in range(size)])  10.7 us
  transfers between devices with their start and end apart: 14, of which 8 were waited for; matrix products, arithmetic and copies ran while one was open for 22% of the time, Pallas kernels for 0%

profile of v1, /device:TPU:0, one launch (start us, length us, event | category | flops | bytes accessed | tf_op | source)
XLA Modules:
  0.0 510.5 jit_solution(13605521798339018455)
XLA Ops:
  14.0 2.6 collective-permute-start.1
  16.7 2.9 collective-permute-done.1
  19.7 2.8 collective-permute-start.2
  22.5 2.3 scatter_custom_fusion.1
  25.9 4.3 all-to-all-start.2
  32.4 7.3 %collective-permute-done.3 = bf16[8,24,768]{2,1,0:T(8,128)(2,1)S(1)} collective-permute-done((bf16[8,24,768]{2,1,0:T(8,128)(2,1)S(1)}, bf16[8,24,768]{2,1,0:T(8,128)(2,1)S(1)}, u32[]{:S(2)}, u32[]{:S(2)}) %collective-permute-start.3) | collective-permute-done | bytes 294944 | tf_op jit(solution)/shard_map/ppermute | solution.py:24
  39.9 1.6 collective-permute-start.4
  43.4 47.9 %all-reduce.18 = (bf16[768]{0:T(1024)(128)(2,1)S(1)}, bf16[768]{0:T(1024)(128)(2,1)S(1)}, bf16[768]{0:T(1024)(128)(2,1)S(1)}, bf16[768]{0:T(1024)(128)(2,1)S(1)}...) all-reduce(bf16[768]{0:T(1024)(128)(2,1)S(1)} %dynamic-update-slice, ...), channel_id=1, replica_groups=mesh['dp'=4,'expert'=8] {'dp','expert'}, use_global_device_ids=true, to_apply=%add.2 | all-reduce | flops 5376 | bytes 21504
  93.0 2.9 fusion.17
  98.0 2.1 fusion.20
  100.3 1.9 convolution_convert_fusion.2
  104.9 2.7 reshape.315
  107.5 2.9 scatter_custom_fusion
  111.4 4.2 all-to-all-start
  117.1 17.3 %all-to-all-done = bf16[8,50,768]{2,1,0:T(8,128)(2,1)} async-done(((bf16[8,50,768]{2,1,0:T(8,128)(2,1)}), bf16[8,50,768]{2,1,0:T(8,128)(2,1)}, u32[]{:S(2)}, u32[]{:S(2)}) %all-to-all-start) | async-done | bytes 614432 | tf_op jit(solution)/shard_map/all_to_all | solution.py:154
  134.5 2.1 reshape.272
  136.5 7.2 %multiply_convert_fusion = (bf16[400,3072]{1,0:T(8,128)(2,1)}, f32[400,3072]{1,0:T(8,128)S(1)}) fusion(f32[3072]{0:T(1024)S(1)} %bitcast.208, bf16[400,768]{1,0:T(8,128)(2,1)} %reshape.272, bf16[1,768,3072]{2,1,0:T(8,128)(2,1)} %param.27), kind=kOutput, calls=%fused_computation.17 | convolution fusion | flops 1899724800 | bytes 12718080 | tf_op jit(solution)/shard_map/dot_general | solution.py:163
  143.7 7.4 %fusion.8 = bf16[400,3072]{1,0:T(8,128)(2,1)S(1)} fusion(f32[400,3072]{1,0:T(8,128)S(1)} %get-tuple-element.93, bf16[400,768]{1,0:T(8,128)(2,1)S(1)} %reshape.278, bf16[1,3072,768]{2,1,0:T(8,128)(2,1)} %param.29, f32[3072]{0:T(1024)S(1)} %bitcast.209), kind=kOutput, calls=%fused_computation.16 | convolution fusion | flops 1913241600 | bytes 12718080 | tf_op jit(solution)/shard_map/dot_general | solution.py:191
  151.2 1.5 copy-done.15
  152.7 4.4 convolution_convert_fusion.1
  157.1 6.7 %convolution_convert_fusion = bf16[3072,768]{1,0:T(8,128)(2,1)} fusion(bf16[400,3072]{1,0:T(8,128)(2,1)} %get-tuple-element.92, bf16[400,768]{1,0:T(8,128)(2,1)S(1)} %reshape.278), kind=kOutput, calls=%fused_computation.8 | convolution fusion | flops 1889796096 | bytes 7790592 | tf_op jit(solution)/shard_map/dot_general | solution.py:202
  163.8 5.2 %fusion.37 = bf16[400,768]{1,0:T(8,128)(2,1)S(1)} fusion(bf16[400,3072]{1,0:T(8,128)(2,1)} %copy-done.15, bf16[1,768,3072]{2,1,0:T(8,128)(2,1)} %param.27), kind=kOutput, calls=%fused_computation.41 | convolution fusion | flops 1887744000 | bytes 7790592 | tf_op jit(solution)/shard_map/dot_general | solution.py:193
  170.1 4.4 all-to-all-start.3
  174.5 5.5 %fusion.34 = bf16[400,768]{1,0:T(8,128)(2,1)S(1)} fusion(bf16[400,3072]{1,0:T(8,128)(2,1)} %get-tuple-element.92, bf16[1,3072,768]{2,1,0:T(8,128)(2,1)} %param.29, f32[768]{0:T(1024)S(1)} %convert_reduce_fusion.2), kind=kOutput, calls=%fused_computation.40 | convolution fusion | flops 1888051200 | bytes 7793664 | tf_op jit(solution)/shard_map/dot_general | solution.py:168
  181.0 12.3 %all-to-all-done.3 = bf16[8,50,768]{2,1,0:T(8,128)(2,1)} async-done(((bf16[8,50,768]{2,1,0:T(8,128)(2,1)}), bf16[8,50,768]{2,1,0:T(8,128)(2,1)}, u32[]{:S(2)}, u32[]{:S(2)}) %all-to-all-start.3) | async-done | bytes 614432 | tf_op jit(solution)/shard_map/all_to_all | solution.py:194
  193.3 4.2 all-to-all-start.1
  199.0 2.7 gather_fusion.1
  201.7 2.8 reshape.290
  204.4 3.6 reduce_sum.214
  208.0 8.4 %all-to-all-done.1 = bf16[8,50,768]{2,1,0:T(8,128)(2,1)} async-done(((bf16[8,50,768]{2,1,0:T(8,128)(2,1)}), bf16[8,50,768]{2,1,0:T(8,128)(2,1)}, u32[]{:S(2)}, u32[]{:S(2)}) %all-to-all-start.1) | async-done | bytes 614432 | tf_op jit(solution)/shard_map/all_to_all | solution.py:171
  217.7 2.7 gather_fusion
  220.3 2.8 reshape.288
  223.1 1.7 multiply_reduce_fusion.2
  224.9 2.8 multiply_reduce_fusion.1
  229.6 1.9 fusion.79
  231.8 2.5 convolution_convert_fusion.3
  235.5 3.1 fusion.28
  238.6 2.1 convolution_bitcast_fusion
  243.1 4.1 fusion.78
  251.0 2.2 reduce_sum.227
  253.2 10.5 %all-reduce.19 = (bf16[3072]{0:T(1024)(128)(2,1)S(1)}, bf16[768]{0:T(1024)(128)(2,1)S(1)}) all-reduce(bf16[3072]{0:T(1024)(128)(2,1)S(1)} %reduce_sum.227, bf16[768]{0:T(1024)(128)(2,1)S(1)} %reduce_sum.228), channel_id=12, replica_groups=mesh['dp'=4,'expert'=8] {'dp'}, use_global_device_ids=true, to_apply=%region_35.36.clone | all-reduce | flops 3840 | bytes 15360
  265.0 3.9 fusion.60
  269.3 1.4 copy.64
  271.1 37.3 %all-reduce.17 = (f32[768]{0:T(1024)S(1)}, f32[768]{0:T(1024)S(1)}, f32[768]{0:T(1024)S(1)}, f32[768]{0:T(1024)S(1)}, f32[768]{0:T(1024)S(1)}, /*index=5*/f32[768]{0:T(1024)S(1)}, f32[768]{0:T(1024)S(1)}) all-reduce(f32[768]{0:T(1024)S(1)} %get-tuple-element.64, ...), channel_id=2, replica_groups=mesh['dp'=4,'expert'=8] {'dp','expert'}, use_global_device_ids=true, to_apply=%region_18.19.clone | all-reduce | flops 5376 | bytes 43008
  312.5 2.9 bitcast_convert_fusion.1
  315.4 2.9 bitcast_convert_fusion
  318.3 60.6 %reduce-scatter.7.cloned.1.call-done = f32[24,768]{1,0:T(8,128)} async-done(((f32[768,768]{1,0:T(8,128)}), f32[24,768]{1,0:T(8,128)}) %reduce-scatter.7.cloned.1.call-update) | async-done | bytes 73744 | tf_op jit(solution)/shard_map/reduce_scatter | solution.py:264
  378.8 124.7 %reduce-scatter.5.cloned.1.call-done = f32[24,2304]{1,0:T(8,128)} async-done(((f32[768,2304]{1,0:T(8,128)}), f32[24,2304]{1,0:T(8,128)}) %reduce-scatter.5.cloned.1.call-update) | async-done | bytes 221200 | tf_op jit(solution)/shard_map/reduce_scatter | solution.py:261
  (187 shorter events, 40.1 us)
Async XLA Ops:
  7.2 85.8 %all-gather.2.cloned.1.call-start = ((), (), s32[]{:S(2)}) async-start(), calls=%async_computation.8 | async-start | bytes 3649536 | tf_op jit(solution)/shard_map/all_gather | solution.py:95
  7.9 6.1 %collective-permute-start = (bf16[1,24,768]{2,1,0:T(8,128)(2,1)}, bf16[1,24,768]{2,1,0:T(8,128)(2,1)S(1)}, u32[]{:S(2)}, u32[]{:S(2)}) collective-permute-start(bf16[1,24,768]{2,1,0:T(8,128)(2,1)} %bitcast.205), channel_id=1, source_target_pairs={{0,1},{1,0},{2,3},{3,2},{4,5},{5,4},{6,7},{7,6},{8,9},{9,8},{10,11... | collective-permute-start | bytes 110600 | tf_op jit(solution)/shard_map/ppermute | solution.py:24
  10.8 2.3 copy-start.22
  12.3 1.4 copy-start.23
  12.3 1.7 copy-start.20
  14.0 5.6 %collective-permute-start.1 = (bf16[2,24,768]{2,1,0:T(8,128)(2,1)S(1)}, bf16[2,24,768]{2,1,0:T(8,128)(2,1)S(1)}, u32[]{:S(2)}, u32[]{:S(2)}) collective-permute-start(bf16[2,24,768]{2,1,0:T(8,128)(2,1)S(1)} %get-tuple-element.89), channel_id=1, source_target_pairs={{0,2},{1,3},{2,0},{3,1},{4,6},{5,7},{6,4},{7,5},{8,10},{9,11},{10,... | collective-permute-start | bytes 221192 | tf_op jit(solution)/shard_map/ppermute | solution.py:24
  19.6 12.7 %copy-start.7 = (bf16[1,197,768]{2,1,0:T(8,128)(2,1)S(1)}, bf16[1,197,768]{2,1,0:T(8,128)(2,1)}, u32[]{:S(2)}) copy-start(bf16[1,197,768]{2,1,0:T(8,128)(2,1)} %param.17) | copy-start | bytes 907780
  19.7 11.1 %collective-permute-start.2 = (bf16[4,24,768]{2,1,0:T(8,128)(2,1)S(1)}, bf16[4,24,768]{2,1,0:T(8,128)(2,1)S(1)}, u32[]{:S(2)}, u32[]{:S(2)}) collective-permute-start(bf16[4,24,768]{2,1,0:T(8,128)(2,1)S(1)} %bitcast.199), channel_id=1, source_target_pairs={{0,4},{1,5},{2,6},{3,7},{4,0},{5,1},{6,2},{7,3},{8,12},{9,13},{10,... | collective-permute-start | bytes 442376 | tf_op jit(solution)/shard_map/ppermute | solution.py:24
  25.9 15.9 %copy-start.25 = (bf16[24]{0:T(256)(128)(2,1)S(1)}, bf16[24]{0:T(256)(128)(2,1)}, u32[]{:S(2)}) copy-start(bf16[24]{0:T(256)(128)(2,1)} %param.19) | copy-start | bytes 148
  25.9 16.1 %copy-start.26 = (bf16[24]{0:T(256)(128)(2,1)S(1)}, bf16[24]{0:T(256)(128)(2,1)}, u32[]{:S(2)}) copy-start(bf16[24]{0:T(256)(128)(2,1)} %param.18) | copy-start | bytes 148
  25.9 16.3 %copy-start.27 = (bf16[24]{0:T(256)(128)(2,1)S(1)}, bf16[24]{0:T(256)(128)(2,1)}, u32[]{:S(2)}) copy-start(bf16[24]{0:T(256)(128)(2,1)} %param.22) | copy-start | bytes 148
  25.9 16.6 %copy-start.28 = (bf16[24]{0:T(256)(128)(2,1)S(1)}, bf16[24]{0:T(256)(128)(2,1)}, u32[]{:S(2)}) copy-start(bf16[24]{0:T(256)(128)(2,1)} %param.21) | copy-start | bytes 148
  25.9 16.8 %copy-start.29 = (bf16[24]{0:T(256)(128)(2,1)S(1)}, bf16[24]{0:T(256)(128)(2,1)}, u32[]{:S(2)}) copy-start(bf16[24]{0:T(256)(128)(2,1)} %param.24) | copy-start | bytes 148
  25.9 17.0 %copy-start.30 = (bf16[24]{0:T(256)(128)(2,1)S(1)}, bf16[24]{0:T(256)(128)(2,1)}, u32[]{:S(2)}) copy-start(bf16[24]{0:T(256)(128)(2,1)} %param.26) | copy-start | bytes 148
  25.9 17.2 %copy-start.31 = (bf16[24]{0:T(256)(128)(2,1)S(1)}, bf16[24]{0:T(256)(128)(2,1)}, u32[]{:S(2)}) copy-start(bf16[24]{0:T(256)(128)(2,1)} %param.25) | copy-start | bytes 148
  25.9 85.5 %all-to-all-start.2 = ((bf16[8,50,768]{2,1,0:T(8,128)(2,1)}), bf16[8,50,768]{2,1,0:T(8,128)(2,1)}, u32[]{:S(2)}, u32[]{:S(2)}) async-start(bf16[8,50,768]{2,1,0:T(8,128)(2,1)} %reshape.277), calls=%async_computation.2 | async-start | bytes 1376256 | tf_op jit(solution)/shard_map/all_to_all | solution.py:184
  30.9 8.9 %collective-permute-start.3 = (bf16[8,24,768]{2,1,0:T(8,128)(2,1)S(1)}, bf16[8,24,768]{2,1,0:T(8,128)(2,1)S(1)}, u32[]{:S(2)}, u32[]{:S(2)}) collective-permute-start(bf16[8,24,768]{2,1,0:T(8,128)(2,1)S(1)} %bitcast.197), channel_id=1, source_target_pairs={{0,8},{1,9},{2,10},{3,11},{4,12},{5,13},{6,14},{7,15},{8,0},{9,1},... | collective-permute-start | bytes 884744 | tf_op jit(solution)/shard_map/ppermute | solution.py:24
  39.9 51.7 %collective-permute-start.4 = (bf16[16,24,768]{2,1,0:T(8,128)(2,1)S(1)}, bf16[16,24,768]{2,1,0:T(8,128)(2,1)S(1)}, u32[]{:S(2)}, u32[]{:S(2)}) collective-permute-start(bf16[16,24,768]{2,1,0:T(8,128)(2,1)S(1)} %bitcast.195), channel_id=1, source_target_pairs={{0,16},{1,17},{2,18},{3,19},{4,20},{5,21},{6,22},{7,23},{8,24},{9,... | collective-permute-start | bytes 1769480 | tf_op jit(solution)/shard_map/ppermute | solution.py:24
  91.5 1.5 copy-start.16
  96.5 1.0 copy-start.2
  100.1 2.0 copy-start.6
  100.3 2.7 copy-start.5
  102.1 2.7 copy-start.13
  102.7 0.8 copy-start
  104.9 11.0 %copy-start.21 = (bf16[1,3072]{1,0:T(2,128)(2,1)S(1)}, bf16[1,3072]{1,0:T(2,128)(2,1)}, u32[]{:S(2)}) copy-start(bf16[1,3072]{1,0:T(2,128)(2,1)} %param.28) | copy-start | bytes 18436
  111.4 23.0 %all-to-all-start = ((bf16[8,50,768]{2,1,0:T(8,128)(2,1)}), bf16[8,50,768]{2,1,0:T(8,128)(2,1)}, u32[]{:S(2)}, u32[]{:S(2)}) async-start(bf16[8,50,768]{2,1,0:T(8,128)(2,1)} %reshape.271), calls=%async_computation | async-start | bytes 1376256 | tf_op jit(solution)/shard_map/all_to_all | solution.py:154
  115.6 196.9 %reduce-scatter.9.cloned.1.call-start = ((), (), s32[]{:S(2)}) async-start(), calls=%async_computation.11 | async-start | bytes 5898240 | tf_op jit(solution)/shard_map/reduce_scatter | solution.py:206
  143.7 8.9 %copy-start.19 = (bf16[400,768]{1,0:T(8,128)(2,1)S(1)}, bf16[400,768]{1,0:T(8,128)(2,1)}, u32[]{:S(2)}) copy-start(bf16[400,768]{1,0:T(8,128)(2,1)} %reshape.272) | copy-start | bytes 1843204
  151.2 1.5 copy-start.15
  157.1 158.3 %reduce-scatter.11.cloned.1.call-start = ((), (), s32[]{:S(2)}) async-start(), calls=%async_computation.12 | async-start | bytes 5898240 | tf_op jit(solution)/shard_map/reduce_scatter | solution.py:209
  169.0 5.5 %copy-start.24 = (bf16[1,768]{1,0:T(2,128)(2,1)S(1)}, bf16[1,768]{1,0:T(2,128)(2,1)}, u32[]{:S(2)}) copy-start(bf16[1,768]{1,0:T(2,128)(2,1)} %param.30) | copy-start | bytes 4612
  170.1 23.3 %all-to-all-start.3 = ((bf16[8,50,768]{2,1,0:T(8,128)(2,1)}), bf16[8,50,768]{2,1,0:T(8,128)(2,1)}, u32[]{:S(2)}, u32[]{:S(2)}) async-start(bf16[8,50,768]{2,1,0:T(8,128)(2,1)} %reshape.279), calls=%async_computation.3 | async-start | bytes 1376256 | tf_op jit(solution)/shard_map/all_to_all | solution.py:194
  193.3 23.1 %all-to-all-start.1 = ((bf16[8,50,768]{2,1,0:T(8,128)(2,1)}), bf16[8,50,768]{2,1,0:T(8,128)(2,1)}, u32[]{:S(2)}, u32[]{:S(2)}) async-start(bf16[8,50,768]{2,1,0:T(8,128)(2,1)} %reshape.273), calls=%async_computation.1 | async-start | bytes 1376256 | tf_op jit(solution)/shard_map/all_to_all | solution.py:171
  197.5 181.3 %reduce-scatter.7.cloned.1.call-start = ((), (), s32[]{:S(2)}) async-start(), calls=%async_computation.10 | async-start | bytes 2433024 | tf_op jit(solution)/shard_map/reduce_scatter | solution.py:264
  220.3 7.4 %copy-start.1 = (f32[197,768]{1,0:T(8,128)S(1)}, f32[197,768]{1,0:T(8,128)}, u32[]{:S(2)}) copy-start(f32[197,768]{1,0:T(8,128)} %copy-done) | copy-start | bytes 1815556
  223.1 4.6 copy-start.8
  223.1 4.6 copy-start.18
  227.7 1.9 copy-start.14
  228.8 0.8 copy-start.10
  231.5 272.0 %reduce-scatter.5.cloned.1.call-start = ((), (), s32[]{:S(2)}) async-start(), calls=%async_computation.9 | async-start | bytes 7299072 | tf_op jit(solution)/shard_map/reduce_scatter | solution.py:261
  238.6 2.1 copy-start.3
  238.6 2.3 copy-start.4
  241.9 1.2 copy-start.17
  242.1 1.0 copy-start.12
  247.2 0.7 copy-start.32
  265.0 4.0 copy-start.11
  269.0 1.8 copy-start.9
Sparse Core Ops, SparseCore 0:
  11.0 67.5 all-gather.1
  157.2 56.1 reduce-scatter.8
  216.4 57.3 reduce-scatter.10
  279.4 99.3 reduce-scatter.6
  384.9 118.5 reduce-scatter.4
